TPU v7x, 32 devices: a whole 2x2x4 slice. The times are simulated.
32 devices in a mesh: section: 8 (over y, x, core), shard: 4 (over z).
Axes of the slice: x: 2, y: 2, z: 4, core: 2. Of those that a mesh axis runs over, the one named last changes fastest.
Arguments:
- kept_slab: bfloat16 [131072, 768], P(('section', 'shard')), may hold values from -1 to 1, as said below
- new_rows: bfloat16 [4, 256, 768], P(None, ('section', 'shard')), may hold values from -1 to 1, as said below
- append_mask: int32 [4, 256], P(None, ('section', 'shard')), may hold values 0 or 1
Outputs:
- maxima: float32 [4, 256], P(None, ('section', 'shard'))
Inputs may be any that keep to these rules, and one draw needn't show every extreme that they name: `kept_slab`: every row has unit Euclidean length up to bfloat16 rounding. `new_rows`: every row has unit Euclidean length up to bfloat16 rounding.
All inputs are finite; a program needn't handle non-finite values. No bound on the sum of `append_mask` on one device may be relied on, other than what follows from the above.
Results may differ from a plain program's by a relative error of at most 0.0003.
Values may be sent and summed in bfloat16 or wider, within the bound.
No kernel may reach another device: no remote copies, remote signals or barrier semaphores. Data moves between devices by JAX's collectives and lax.ppermute only.
A program may use at most 64 MiB of HBM per device.

v0:
```python
import jax
import jax.numpy as jnp
from jax import lax
from jax.sharding import PartitionSpec as P


def per_device(kept_slab, new_rows, append_mask):
    micro_count = new_rows.shape[0]
    own_count = new_rows.shape[1]
    width = new_rows.shape[2]
    devices_total = lax.axis_size("section") * lax.axis_size("shard")
    batch_rows = own_count * devices_total
    append_flags = append_mask.astype(jnp.bfloat16)
    gathered_rows, gathered_flags = (
        lax.all_gather(new_rows, ("section", "shard"), axis=1, tiled=True),
        lax.all_gather(append_flags, ("section", "shard"), axis=1, tiled=True),
    )
    flattened = gathered_rows.reshape(micro_count * batch_rows, width)
    slab_rows = kept_slab.shape[0]
    block_rows = min(512, slab_rows)
    kept_blocks = kept_slab.reshape(slab_rows // block_rows, block_rows, width)

    def visit(highest, block):
        scores = lax.dot_general(
            flattened, block, (((1,), (1,)), ((), ())), preferred_element_type=jnp.float32
        )
        return (jnp.maximum(highest, jnp.max(scores, axis=1)), None)

    slab_flat, _ = lax.scan(
        visit, jnp.full((micro_count * batch_rows,), -3.0, jnp.float32), kept_blocks
    )
    slab_state = slab_flat.reshape(micro_count, batch_rows)
    later = lax.broadcasted_iota(
        jnp.int32, (micro_count, 1, micro_count, 1), 0
    ) > lax.broadcasted_iota(jnp.int32, (micro_count, 1, micro_count, 1), 2)
    cross = jnp.einsum("qid,kjd->qikj", new_rows, gathered_rows, preferred_element_type=jnp.float32)
    usable = later & (gathered_flags[None, None, :, :] > 0.5)
    stream_state = jnp.max(jnp.where(usable, cross, jnp.float32(-3.0)), axis=(2, 3))
    received = lax.all_to_all(
        slab_state, ("section", "shard"), split_axis=1, concat_axis=0, tiled=True
    )
    own_slab = jnp.max(received.reshape(devices_total, micro_count, own_count), axis=0)
    return jnp.maximum(own_slab, stream_state)


def solution(mesh):
    return jax.shard_map(
        per_device,
        mesh=mesh,
        in_specs=(
            P(("section", "shard"), None),
            P(None, ("section", "shard"), None),
            P(None, ("section", "shard")),
        ),
        out_specs=P(None, ("section", "shard")),
        check_vma=False,
    )
```

profile of v0, /device:TPU:0, one launch (start us, length us, event | category | flops | bytes accessed | tf_op | source)
XLA Modules:
  0.0 118.4 jit_solution(1405508363463907266)
XLA Ops:
  6.5 0.0 all-gather.3.cloned.1.call-start
  6.5 0.7 all-gather.3.cloned.1.call-update
  7.3 0.7 convert_bitcast_fusion
  8.0 70.0 %all-gather = bf16[32,8,4]{1,2,0:T(4,128)(2,1)S(1)} all-gather(bf16[1,8,4]{1,2,0:T(4,128)(2,1)S(1)} %convert_bitcast_fusion), channel_id=1, replica_groups=mesh['section'=8,'shard'=4] {'section','shard'}, dimensions={0}, use_global_device_ids=true | all-gather | bytes 2112 | tf_op jit(solution)/shard_map/all_gather | solution.py:16
  78.0 0.1 copy.8
  78.1 0.1 copy.9
  78.2 0.1 reshape.34
  78.3 0.1 broadcast_and_fusion
  78.4 0.0 all-gather.3.cloned.1.call-done
  78.4 0.0 copy-start
  78.4 21.7 %while.11 = (s32[]{:T(128)}, f32[1024]{0:T(1024)S(1)}, bf16[8,512,768]{2,1,0:T(8,128)(2,1)}, bf16[1024,768]{1,0:T(8,128)(2,1)}, s32[]{:T(128)}, /*index=5*/s32[]{:T(128)}) while((s32[]{:T(128)}, f32[1024]{0:T(1024)S(1)}, bf16[8,512,768]{2,1,0:T(8,128)(2,1)}, bf16[1024,768]{1,0:T(8,128)(2,1)}, s32[]{:T(128)}, ...), condition=%wide.region_2.3_spmd.clone, body=%wide.region_0.2_spmd.clone.sunk | while | flops 805831680 | bytes 2375771 | solution.py:29
  78.4 2.7 %convolution_reduce_fusion.2 = f32[1024]{0:T(1024)S(1)} fusion(bf16[1024,768]{1,0:T(8,128)(2,1)} %get-tuple-element.91, bf16[8,512,768]{2,1,0:T(8,128)(2,1)} %get-tuple-element.90, s32[]{:T(128)S(6)} %copy.13), kind=kOutput, calls=%fused_computation.clone.1 | convolution fusion | flops 805829632 | bytes 2363396 | tf_op jit(solution)/shard_map/while/body/eval_jaxpr/dot_general | solution.py:24
  81.1 2.7 %convolution_reduce_fusion.2 = f32[1024]{0:T(1024)S(1)} fusion(bf16[1024,768]{1,0:T(8,128)(2,1)} %get-tuple-element.91, bf16[8,512,768]{2,1,0:T(8,128)(2,1)} %get-tuple-element.90, s32[]{:T(128)S(6)} %copy.13), kind=kOutput, calls=%fused_computation.clone.1 | convolution fusion | flops 805829632 | bytes 2363396 | tf_op jit(solution)/shard_map/while/body/eval_jaxpr/dot_general | solution.py:24
  83.9 2.7 %convolution_reduce_fusion.2 = f32[1024]{0:T(1024)S(1)} fusion(bf16[1024,768]{1,0:T(8,128)(2,1)} %get-tuple-element.91, bf16[8,512,768]{2,1,0:T(8,128)(2,1)} %get-tuple-element.90, s32[]{:T(128)S(6)} %copy.13), kind=kOutput, calls=%fused_computation.clone.1 | convolution fusion | flops 805829632 | bytes 2363396 | tf_op jit(solution)/shard_map/while/body/eval_jaxpr/dot_general | solution.py:24
  86.6 2.7 %convolution_reduce_fusion.2 = f32[1024]{0:T(1024)S(1)} fusion(bf16[1024,768]{1,0:T(8,128)(2,1)} %get-tuple-element.91, bf16[8,512,768]{2,1,0:T(8,128)(2,1)} %get-tuple-element.90, s32[]{:T(128)S(6)} %copy.13), kind=kOutput, calls=%fused_computation.clone.1 | convolution fusion | flops 805829632 | bytes 2363396 | tf_op jit(solution)/shard_map/while/body/eval_jaxpr/dot_general | solution.py:24
  89.3 2.7 %convolution_reduce_fusion.2 = f32[1024]{0:T(1024)S(1)} fusion(bf16[1024,768]{1,0:T(8,128)(2,1)} %get-tuple-element.91, bf16[8,512,768]{2,1,0:T(8,128)(2,1)} %get-tuple-element.90, s32[]{:T(128)S(6)} %copy.13), kind=kOutput, calls=%fused_computation.clone.1 | convolution fusion | flops 805829632 | bytes 2363396 | tf_op jit(solution)/shard_map/while/body/eval_jaxpr/dot_general | solution.py:24
  92.0 2.7 %convolution_reduce_fusion.2 = f32[1024]{0:T(1024)S(1)} fusion(bf16[1024,768]{1,0:T(8,128)(2,1)} %get-tuple-element.91, bf16[8,512,768]{2,1,0:T(8,128)(2,1)} %get-tuple-element.90, s32[]{:T(128)S(6)} %copy.13), kind=kOutput, calls=%fused_computation.clone.1 | convolution fusion | flops 805829632 | bytes 2363396 | tf_op jit(solution)/shard_map/while/body/eval_jaxpr/dot_general | solution.py:24
  94.7 2.7 %convolution_reduce_fusion.2 = f32[1024]{0:T(1024)S(1)} fusion(bf16[1024,768]{1,0:T(8,128)(2,1)} %get-tuple-element.91, bf16[8,512,768]{2,1,0:T(8,128)(2,1)} %get-tuple-element.90, s32[]{:T(128)S(6)} %copy.13), kind=kOutput, calls=%fused_computation.clone.1 | convolution fusion | flops 805829632 | bytes 2363396 | tf_op jit(solution)/shard_map/while/body/eval_jaxpr/dot_general | solution.py:24
  97.4 2.7 %convolution_reduce_fusion.2 = f32[1024]{0:T(1024)S(1)} fusion(bf16[1024,768]{1,0:T(8,128)(2,1)} %get-tuple-element.91, bf16[8,512,768]{2,1,0:T(8,128)(2,1)} %get-tuple-element.90, s32[]{:T(128)S(6)} %copy.13), kind=kOutput, calls=%fused_computation.clone.1 | convolution fusion | flops 805829632 | bytes 2363396 | tf_op jit(solution)/shard_map/while/body/eval_jaxpr/dot_general | solution.py:24
  100.1 0.1 all_to_all.10
  100.2 0.7 copy.7
  100.9 2.5 %all-to-all-start = ((f32[4,32,8]{2,0,1:T(4,128)}), f32[4,32,8]{2,0,1:T(4,128)S(1)}, u32[]{:S(2)}, u32[]{:S(2)}) async-start(f32[4,32,8]{2,0,1:T(4,128)} %copy.7), calls=%async_computation | async-start | bytes 131072 | tf_op jit(solution)/shard_map/all_to_all | solution.py:39
  103.4 0.0 copy-done
  103.4 2.1 %fusion.8 = f32[4,8]{1,0:T(4,128)S(1)} fusion(bf16[4,256,768]{2,1,0:T(8,128)(2,1)} %bitcast.30, pred[4,4,256]{2,1,0:T(4,128)(4,1)S(1)} %broadcast_and_fusion, bf16[4,8,768]{2,1,0:T(8,128)(2,1)S(1)} %copy-done), kind=kOutput, calls=%fused_computation.8 | convolution fusion | flops 50397152 | bytes 1626240 | tf_op jit(solution)/shard_map/qid,kjd->qikj/dot_general | solution.py:36
  105.5 5.4 %all-to-all-done = f32[4,32,8]{2,0,1:T(4,128)S(1)} async-done(((f32[4,32,8]{2,0,1:T(4,128)}), f32[4,32,8]{2,0,1:T(4,128)S(1)}, u32[]{:S(2)}, u32[]{:S(2)}) %all-to-all-start) | async-done | bytes 4128 | tf_op jit(solution)/shard_map/all_to_all | solution.py:39
  111.0 0.6 max.6
  (12 shorter events, 0.1 us)
Async XLA Ops:
  6.5 71.9 %all-gather.3.cloned.1.call-start = ((), (), s32[]{:S(2)}) async-start(), calls=%async_computation.1 | async-start | bytes 1622016 | tf_op jit(solution)/shard_map/all_gather | solution.py:15
  78.4 25.0 %copy-start = (bf16[4,8,768]{2,1,0:T(8,128)(2,1)S(1)}, bf16[4,8,768]{2,1,0:T(8,128)(2,1)}, u32[]{:S(2)}) copy-start(bf16[4,8,768]{2,1,0:T(8,128)(2,1)} %param.6) | copy-start | bytes 147460
  100.9 10.1 %all-to-all-start = ((f32[4,32,8]{2,0,1:T(4,128)}), f32[4,32,8]{2,0,1:T(4,128)S(1)}, u32[]{:S(2)}, u32[]{:S(2)}) async-start(f32[4,32,8]{2,0,1:T(4,128)} %copy.7), calls=%async_computation | async-start | bytes 131072 | tf_op jit(solution)/shard_map/all_to_all | solution.py:39
Sparse Core Ops, SparseCore 0:
  10.2 55.3 all-gather.2
where the time goes:
time: 119 us; the launch traced here: 118 us
  blocking collectives  70 us (59%)
  matrix products  23.4 us (20%)
  between operations  13.5 us (11%)
  waiting for transfers between devices  6.15 us (5%)
  starting transfers between devices  2.55 us (2%)
  other arithmetic  1.46 us (1%)
    all_gather x1, blocking collectives, per_device(): lax.all_gather(append_flags, ('section', 'shard'), axis=1, tiled=True)  70 us
    dot_general x8, matrix products, visit(): lax.dot_general(flattened, block, (((1,), (1,)), ((), ())), preferred_ele...  21.4 us
    all_to_all x1, waiting for transfers between devices, per_device(): lax.all_to_all(slab_state, ('section', 'shard'), split_axis=1, concat_axi...  5.44 us
    all_to_all x1, starting transfers between devices, per_device(): lax.all_to_all(slab_state, ('section', 'shard'), split_axis=1, concat_axi...  2.55 us
  transfers between devices with their start and end apart: 2, of which 1 were waited for; matrix products, arithmetic and copies ran while one was open for 3% of the time, Pallas kernels for 0%

commit v1 on v0

v1 whole, which is shorter than its diff:
```python
import functools

import jax
import jax.numpy as jnp
from jax import lax
from jax.experimental import pallas as pl
from jax.experimental.pallas import tpu as pltpu
from jax.sharding import PartitionSpec as P

AXES = ("section", "shard")
LANES = 128
NONE_YET = -3.0


def partner_mask(mesh):
    columns = mesh.shape["shard"]
    devices = mesh.devices
    here, beside = devices[0, 0], devices[0, 1 % columns]
    if columns > 1 and getattr(here, "coords", 0) == getattr(beside, "coords", 1):
        return 1
    return columns


def masks_of(mesh):
    columns, total = mesh.shape["shard"], mesh.size
    pair = partner_mask(mesh)
    inner = [m for m in range(1, columns) if not m & pair]
    outer = [m for m in range(columns, total, columns) if not m & pair]
    return pair, inner, outer


def swap(rows, mask, total):
    return lax.ppermute(rows, AXES, [(i, i ^ mask) for i in range(total)])


def best_of(kept_ref, own_ref, flag_ref, queries, micro_count, own_count):
    count = queries.shape[0]
    contract = (((1,), (1,)), ((), ()))
    tile = min(512, kept_ref.shape[0])
    best = jnp.full((8, count), NONE_YET, jnp.float32)
    for start in range(0, kept_ref.shape[0], tile):
        scores = lax.dot_general(
            kept_ref[start : start + tile, :], queries, contract, preferred_element_type=jnp.float32
        )
        best = jnp.maximum(best, jnp.max(scores.reshape(tile // 8, 8, count), axis=0))
    block = micro_count * own_count
    cross = lax.dot_general(own_ref[...], queries, contract, preferred_element_type=jnp.float32)
    row = lax.broadcasted_iota(jnp.int32, (block, count), 0)
    column = lax.broadcasted_iota(jnp.int32, (block, count), 1)
    earlier = row // own_count < (column % block) // own_count
    usable = earlier & (flag_ref[...] == 1)
    cross = jnp.where(usable, cross, NONE_YET)
    best = jnp.maximum(best, jnp.max(cross.reshape(block // 8, 8, count), axis=0))
    return jnp.max(best, axis=0, keepdims=True)


def chunk_kernel(parts, micro_count, own_count, kept_ref, own_ref, flag_ref, *refs):
    queries = jnp.concatenate([r[...] for r in refs[:parts]], axis=0)
    refs[parts][...] = best_of(kept_ref, own_ref, flag_ref, queries, micro_count, own_count)


def last_kernel(parts, masks, micro_count, own_count, kept_ref, own_ref, flag_ref, *refs):
    queries = jnp.concatenate([r[...] for r in refs[:parts]], axis=0)
    *earlier, out_ref = refs[parts:]
    block = micro_count * own_count
    me = lax.axis_index(AXES[0]) * lax.axis_size(AXES[1]) + lax.axis_index(AXES[1])
    last = best_of(kept_ref, own_ref, flag_ref, queries, micro_count, own_count)
    for best, owners in zip([r[...] for r in earlier] + [last], masks, strict=True):
        short = -best.shape[1] % LANES
        if short:
            best = jnp.concatenate([best, jnp.zeros((1, short), best.dtype)], axis=1)
        for at, mask in enumerate(owners):
            start = at * block
            base = start // LANES * LANES
            piece = best[:, base : base + LANES]
            if start - base:
                piece = pltpu.roll(piece, LANES - (start - base), 1)
            out_ref[jnp.bitwise_xor(me, mask)] = piece


def per_device(mesh, kept_slab, new_rows, append_mask):
    micro_count, own_count, width = new_rows.shape
    block = micro_count * own_count
    total = mesh.size
    pair, inner, outer = masks_of(mesh)
    own = new_rows.reshape(block, width)
    flags = append_mask.reshape(block, 1)
    shared = (kept_slab, own, flags)
    vmem = pl.BlockSpec(memory_space=pltpu.VMEM)

    def params(rows):
        return dict(
            compiler_params=pltpu.CompilerParams(vmem_limit_bytes=24 * 2**20),
            cost_estimate=pl.CostEstimate(
                flops=2 * rows * kept_slab.shape[0] * width,
                bytes_accessed=2 * kept_slab.shape[0] * width,
                transcendentals=0,
            ),
        )

    def chunk(*parts):
        rows = sum(p.shape[0] for p in parts)
        return pl.pallas_call(
            functools.partial(chunk_kernel, len(parts), micro_count, own_count),
            out_shape=jax.ShapeDtypeStruct((1, rows), jnp.float32),
            in_specs=[vmem] * (3 + len(parts)),
            out_specs=vmem,
            **params(rows),
        )(*shared, *parts)

    def last(parts, bests, masks):
        rows = sum(p.shape[0] for p in parts)
        return pl.pallas_call(
            functools.partial(last_kernel, len(parts), masks, micro_count, own_count),
            out_shape=jax.ShapeDtypeStruct((total, 1, LANES), jnp.float32),
            in_specs=[vmem] * (3 + len(parts) + len(bests)),
            out_specs=vmem,
            **params(rows),
        )(*shared, *parts, *bests)

    z = [swap(own, m, total) for m in inner]
    p = [swap(own, m, total) for m in outer]
    z_all = jnp.concatenate(z, axis=0)
    near = [0, *outer, *inner]
    near_all = jnp.concatenate([own, *p, *z], axis=0)
    near_pair = swap(near_all, pair, total)
    far = [swap(z_all, m, total) for m in outer]
    far_pair = [swap(f, pair, total) for f in far]

    bests, masks = [], []
    bests.append(chunk(near_all))
    masks.append(near)
    bests.append(chunk(near_pair))
    masks.append([m ^ pair for m in near])
    far_masks = [[o ^ i for i in inner] for o in outer]
    for mine, theirs, owners in zip(far[:-1], far_pair[:-1], far_masks[:-1], strict=True):
        bests.append(chunk(mine, theirs))
        masks.append(owners + [m ^ pair for m in owners])
    masks.append(far_masks[-1] + [m ^ pair for m in far_masks[-1]])
    partial = last([far[-1], far_pair[-1]], bests, masks)
    received = lax.all_to_all(partial, AXES, split_axis=0, concat_axis=0, tiled=True)
    return jnp.max(received[:, 0, :block], axis=0).reshape(micro_count, own_count)


def solution(mesh):
    return jax.shard_map(
        functools.partial(per_device, mesh),
        mesh=mesh,
        in_specs=(
            P(AXES, None),
            P(None, AXES, None),
            P(None, AXES),
        ),
        out_specs=P(None, AXES),
        check_vma=False,
    )
```

time: 119 us -> 47.8 us (0.40)
  blocking collectives: 70 us -> 9.22 us
  matrix products: 23.4 us -> 0 us
  between operations: 13.5 us -> 0.13 us
  starting transfers between devices: 2.55 us -> 13.8 us
  Pallas kernels: 0 us -> 9.54 us
  local copies, waits for them, and re-layouts: 1.05 us -> 5.88 us
  waiting for transfers between devices: 6.15 us -> 8.91 us
  other arithmetic: 1.46 us -> 0.05 us
    all_gather x1 -> x0, blocking collectives: 70 us -> none  [per_device(): lax.all_gather(append_flags, ('section', 'shard'), axis=1, tiled=True)]
    dot_general x9 -> x0, matrix products: 23.4 us -> none  [the longest x8 21.4 us: visit(): lax.dot_general(flattened, block, (((1,), (1,)), ((), ())), preferred_ele...]
    ppermute x0 -> x13, starting transfers between devices: none -> 13.8 us  [swap(): return lax.ppermute(rows, AXES, [(i, i ^ mask) for i in range(total)])]
    pallas_call x0 -> x5, Pallas kernels: none -> 9.54 us  [the longest x4 7.59 us: chunk(): pl.pallas_call(functools.partial(chunk_kernel, len(parts), micro_count, o...]
    all_to_all x0 -> x1, blocking collectives: none -> 9.22 us  [per_device(): lax.all_to_all(partial, AXES, split_axis=0, concat_axis=0, tiled=True)]
    ppermute x0 -> x13, waiting for transfers between devices: none -> 8.91 us  [swap(): return lax.ppermute(rows, AXES, [(i, i ^ mask) for i in range(total)])]
    all_to_all x1 -> x0, waiting for transfers between devices: 5.44 us -> none  [per_device(): lax.all_to_all(slab_state, ('section', 'shard'), split_axis=1, concat_axi...]
    unnamed x2 -> x10, local copies, waits for them, and re-layouts: 0.01 us -> 4.45 us
  transfers between devices with their start and end apart: 2 -> 13, of which waited for: 1 -> 3; matrix products, arithmetic and copies ran while one was open for 3% -> 3% of each run, Pallas kernels for 0% -> 16%
where the time goes in v1:
time: 47.8 us; the launch traced here: 47.5 us
  starting transfers between devices  13.8 us (29%)
  Pallas kernels  9.54 us (20%)
  blocking collectives  9.22 us (19%)
  waiting for transfers between devices  8.91 us (19%)
  local copies, waits for them, and re-layouts  5.88 us (12%)
    ppermute x13, starting transfers between devices, swap(): return lax.ppermute(rows, AXES, [(i, i ^ mask) for i in range(total)])  13.8 us
    all_to_all x1, blocking collectives, per_device(): lax.all_to_all(partial, AXES, split_axis=0, concat_axis=0, tiled=True)  9.22 us
    ppermute x13, waiting for transfers between devices, swap(): return lax.ppermute(rows, AXES, [(i, i ^ mask) for i in range(total)])  8.91 us
    pallas_call x4, Pallas kernels, chunk(): pl.pallas_call(functools.partial(chunk_kernel, len(parts), micro_count, o...  7.59 us
    unnamed x10, local copies, waits for them, and re-layouts  4.45 us
    pallas_call x1, Pallas kernels, last(): pl.pallas_call(functools.partial(last_kernel, len(parts), masks, micro_co...  1.96 us
  transfers between devices with their start and end apart: 13, of which 3 were waited for; matrix products, arithmetic and copies ran while one was open for 3% of the time, Pallas kernels for 16%

profile of v1, /device:TPU:0, one launch (start us, length us, event | category | flops | bytes accessed | tf_op | source)
XLA Modules:
  0.0 47.5 jit_solution(11559588927132157951)
XLA Ops:
  0.0 3.0 %collective-permute-start.5 = (bf16[32,768]{1,0:T(8,128)(2,1)}, bf16[32,768]{1,0:T(8,128)(2,1)S(1)}, u32[]{:S(2)}, u32[]{:S(2)}) collective-permute-start(bf16[32,768]{1,0:T(8,128)(2,1)} %bitcast.2), channel_id=1, source_target_pairs={{0,8},{1,9},{2,10},{3,11},{4,12},{5,13},{6,14},{7,15},{8,0},{9,1},... | collective-permute-start | bytes 147464 | tf_op jit(solution)/shard_map/ppermute | solution.py:33
  3.0 1.5 %collective-permute-start.6 = (bf16[32,768]{1,0:T(8,128)(2,1)}, bf16[32,768]{1,0:T(8,128)(2,1)S(1)}, u32[]{:S(2)}, u32[]{:S(2)}) collective-permute-start(bf16[32,768]{1,0:T(8,128)(2,1)} %bitcast.3), channel_id=1, source_target_pairs={{0,16},{1,17},{2,18},{3,19},{4,20},{5,21},{6,22},{7,23},{8,24},{9,... | collective-permute-start | bytes 147464 | tf_op jit(solution)/shard_map/ppermute | solution.py:33
  4.5 0.0 collective-permute-start.7
  4.5 2.1 %collective-permute-start = (bf16[32,768]{1,0:T(8,128)(2,1)}, bf16[32,768]{1,0:T(8,128)(2,1)S(1)}, u32[]{:S(2)}, u32[]{:S(2)}) collective-permute-start(bf16[32,768]{1,0:T(8,128)(2,1)} %bitcast.5), channel_id=1, source_target_pairs={{0,1},{1,0},{2,3},{3,2},{4,5},{5,4},{6,7},{7,6},{8,9},{9,8},{10,11... | collective-permute-start | bytes 147464 | tf_op jit(solution)/shard_map/ppermute | solution.py:33
  6.5 2.6 %collective-permute-start.1 = (bf16[32,768]{1,0:T(8,128)(2,1)}, bf16[32,768]{1,0:T(8,128)(2,1)S(1)}, u32[]{:S(2)}, u32[]{:S(2)}) collective-permute-start(bf16[32,768]{1,0:T(8,128)(2,1)} %bitcast.6), channel_id=1, source_target_pairs={{0,2},{1,3},{2,0},{3,1},{4,6},{5,7},{6,4},{7,5},{8,10},{9,11},{10,... | collective-permute-start | bytes 147464 | tf_op jit(solution)/shard_map/ppermute | solution.py:33
  9.1 0.8 %constant_dynamic-update-slice_fusion.9 = bf16[224,768]{1,0:T(8,128)(2,1)S(1)} fusion(bf16[4,8,768]{2,1,0:T(8,128)(2,1)} %param.4), kind=kLoop, calls=%fused_computation.9 | loop fusion | bytes 98304
  10.0 0.0 collective-permute-done.5
  10.0 0.0 collective-permute-start.2
  10.0 0.0 collective-permute-done.7
  10.1 2.6 %collective-permute-done.1 = bf16[32,768]{1,0:T(8,128)(2,1)S(1)} collective-permute-done((bf16[32,768]{1,0:T(8,128)(2,1)}, bf16[32,768]{1,0:T(8,128)(2,1)S(1)}, u32[]{:S(2)}, u32[]{:S(2)}) %collective-permute-start.1) | collective-permute-done | bytes 49184 | tf_op jit(solution)/shard_map/ppermute | solution.py:33
  12.7 3.4 %collective-permute-done.2 = bf16[32,768]{1,0:T(8,128)(2,1)S(1)} collective-permute-done((bf16[32,768]{1,0:T(8,128)(2,1)}, bf16[32,768]{1,0:T(8,128)(2,1)S(1)}, u32[]{:S(2)}, u32[]{:S(2)}) %collective-permute-start.2) | collective-permute-done | bytes 49184 | tf_op jit(solution)/shard_map/ppermute | solution.py:33
  16.1 1.6 %collective-permute-start.11 = (bf16[96,768]{1,0:T(8,128)(2,1)S(1)}, bf16[96,768]{1,0:T(8,128)(2,1)S(1)}, u32[]{:S(2)}, u32[]{:S(2)}) collective-permute-start(bf16[96,768]{1,0:T(8,128)(2,1)S(1)} %get-tuple-element.6), channel_id=1, source_target_pairs={{0,16},{1,17},{2,18},{3,19},{4,20},{5,21},{6,22},{7,23},{8,24},{9,... | collective-permute-start | bytes 442376 | tf_op jit(solution)/shard_map/ppermute | solution.py:33
  17.7 1.5 %collective-permute-start.9 = (bf16[96,768]{1,0:T(8,128)(2,1)S(1)}, bf16[96,768]{1,0:T(8,128)(2,1)S(1)}, u32[]{:S(2)}, u32[]{:S(2)}) collective-permute-start(bf16[96,768]{1,0:T(8,128)(2,1)S(1)} %get-tuple-element.6), channel_id=1, source_target_pairs={{0,8},{1,9},{2,10},{3,11},{4,12},{5,13},{6,14},{7,15},{8,0},{9,1},... | collective-permute-start | bytes 442376 | tf_op jit(solution)/shard_map/ppermute | solution.py:33
  19.2 0.5 %collective-permute-start.3 = (bf16[96,768]{1,0:T(8,128)(2,1)S(1)}, bf16[96,768]{1,0:T(8,128)(2,1)S(1)}, u32[]{:S(2)}, u32[]{:S(2)}) collective-permute-start(bf16[96,768]{1,0:T(8,128)(2,1)S(1)} %get-tuple-element.6), channel_id=1, source_target_pairs={{0,24},{1,25},{2,26},{3,27},{4,28},{5,29},{6,30},{7,31},{8,16},{9,... | collective-permute-start | bytes 442376 | tf_op jit(solution)/shard_map/ppermute | solution.py:33
  19.6 2.9 %collective-permute-done.11.refs_0_ = bf16[96,768]{1,0:T(8,128)(2,1)S(1)} collective-permute-done((bf16[96,768]{1,0:T(8,128)(2,1)S(1)}, bf16[96,768]{1,0:T(8,128)(2,1)S(1)}, u32[]{:S(2)}, u32[]{:S(2)}) %collective-permute-start.11) | collective-permute-done | bytes 147488 | tf_op jit(solution)/shard_map/ppermute | solution.py:33
  22.5 0.0 collective-permute-start.12
  22.5 0.8 %reshape.12.flag_ref = s32[32,1]{1,0:T(8,128)S(1)} reshape(s32[4,8]{1,0:T(4,128)} %param.5) | data formatting | bytes 256 | tf_op jit(solution)/shard_map/reshape | solution.py:87
  23.3 0.5 %collective-permute-start.8 = (bf16[224,768]{1,0:T(8,128)(2,1)S(1)}, bf16[224,768]{1,0:T(8,128)(2,1)S(1)}, u32[]{:S(2)}, u32[]{:S(2)}) collective-permute-start(bf16[224,768]{1,0:T(8,128)(2,1)S(1)} %get-tuple-element.5.refs_0_), channel_id=1, source_target_pairs={{0,4},{1,5},{2,6},{3,7},{4,0},{5,1},{6,2},{7,3},{8,12},{9,13},{10,... | collective-permute-start | bytes 1032200 | tf_op jit(solution)/shard_map/ppermute | solution.py:33
  23.8 0.1 collective-permute-start.10
  23.9 2.8 %copy-done = bf16[4096,768]{1,0:T(8,128)(2,1)S(1)} copy-done((bf16[4096,768]{1,0:T(8,128)(2,1)S(1)}, bf16[4096,768]{1,0:T(8,128)(2,1)}, u32[]{:S(2)}) %copy-start) | copy-done | bytes 6291480
  26.7 0.8 %copy-done.1 = bf16[4,8,768]{2,1,0:T(8,128)(2,1)S(1)} copy-done((bf16[4,8,768]{2,1,0:T(8,128)(2,1)S(1)}, bf16[4,8,768]{2,1,0:T(8,128)(2,1)}, u32[]{:S(2)}) %copy-start.1) | copy-done | bytes 49176
  27.5 1.9 %shard_map.37.refs_2_ = f32[1,224]{1,0:T(1,128)S(1)} custom-call(bf16[4096,768]{1,0:T(8,128)(2,1)S(1)} %copy-done, bf16[32,768]{1,0:T(8,128)(2,1)S(1)} %bitcast.8, s32[32,1]{1,0:T(8,128)S(1)} %reshape.12.flag_ref, bf16[224,768]{1,0:T(8,128)(2,1)S(1)} %get-tuple-element.5.refs_0_), custom_call_target="tpu_custom_call" | custom-call | flops 1409286144 | bytes 6291456 | tf_op jit(solution)/shard_map/pallas_call | solution.py:103
  29.4 0.5 %collective-permute-start.4 = (bf16[96,768]{1,0:T(8,128)(2,1)S(1)}, bf16[96,768]{1,0:T(8,128)(2,1)S(1)}, u32[]{:S(2)}, u32[]{:S(2)}) collective-permute-start(bf16[96,768]{1,0:T(8,128)(2,1)S(1)} %collective-permute-done.3.refs_0_), channel_id=1, source_target_pairs={{0,4},{1,5},{2,6},{3,7},{4,0},{5,1},{6,2},{7,3},{8,12},{9,13},{10,... | collective-permute-start | bytes 442376 | tf_op jit(solution)/shard_map/ppermute | solution.py:33
  29.9 0.0 collective-permute-done.12.refs_1_
  29.9 1.9 %shard_map.40.refs_5_ = f32[1,192]{1,0:T(1,128)S(1)} custom-call(bf16[4096,768]{1,0:T(8,128)(2,1)S(1)} %copy-done, bf16[32,768]{1,0:T(8,128)(2,1)S(1)} %bitcast.9, s32[32,1]{1,0:T(8,128)S(1)} %reshape.12.flag_ref, bf16[96,768]{1,0:T(8,128)(2,1)S(1)} %collective-permute-done.11.refs_0_, bf16[96,768]{1,0:T(8,128)(2,1)S(1)} %collective-permute-done.12.refs_1_), custom_call_target="tpu_custom_call" | custom-call | flops 1207959552 | bytes 6291456 | tf_op jit(solution)/shard_map/pallas_call | solution.py:103
  31.8 0.0 collective-permute-done.10.refs_1_
  31.8 1.9 %shard_map.39.refs_4_ = f32[1,192]{1,0:T(1,128)S(1)} custom-call(bf16[4096,768]{1,0:T(8,128)(2,1)S(1)} %copy-done, bf16[32,768]{1,0:T(8,128)(2,1)S(1)} %bitcast.10, s32[32,1]{1,0:T(8,128)S(1)} %reshape.12.flag_ref, bf16[96,768]{1,0:T(8,128)(2,1)S(1)} %collective-permute-done.9.refs_0_, bf16[96,768]{1,0:T(8,128)(2,1)S(1)} %collective-permute-done.10.refs_1_), custom_call_target="tpu_custom_call" | custom-call | flops 1207959552 | bytes 6291456 | tf_op jit(solution)/shard_map/pallas_call | solution.py:103
  33.7 1.9 %shard_map.38.refs_3_ = f32[1,224]{1,0:T(1,128)S(1)} custom-call(bf16[4096,768]{1,0:T(8,128)(2,1)S(1)} %copy-done, bf16[32,768]{1,0:T(8,128)(2,1)S(1)} %bitcast.11, s32[32,1]{1,0:T(8,128)S(1)} %reshape.12.flag_ref, bf16[224,768]{1,0:T(8,128)(2,1)S(1)} %collective-permute-done.8.refs_0_), custom_call_target="tpu_custom_call" | custom-call | flops 1409286144 | bytes 6291456 | tf_op jit(solution)/shard_map/pallas_call | solution.py:103
  35.6 2.0 %shard_map.41 = f32[32,1,128]{2,1,0:T(1,128)S(1)} custom-call(bf16[4096,768]{1,0:T(8,128)(2,1)S(1)} %copy-done, bf16[32,768]{1,0:T(8,128)(2,1)S(1)} %bitcast.12, s32[32,1]{1,0:T(8,128)S(1)} %reshape.12.flag_ref, bf16[96,768]{1,0:T(8,128)(2,1)S(1)} %collective-permute-done.3.refs_0_, bf16[96,768]{1,0:T(8,128)(2,1)S(1)} %collective-permute-done.4.refs_1_, ...), custom_call_target="tpu_custom_call" | custom-call | flops 1207959552 | bytes 6291456 | tf_op jit(solution)/shard_map/pallas_call | solution.py:113
  37.6 9.2 %all_to_all.5 = f32[32,1,128]{2,1,0:T(1,128)S(1)} all-to-all(f32[32,1,128]{2,1,0:T(1,128)S(1)} %shard_map.41), channel_id=1, replica_groups=mesh['section'=8,'shard'=4] {'section','shard'}, dimensions={0} | all-to-all | bytes 32768 | tf_op jit(solution)/shard_map/all_to_all | solution.py:141
  46.8 0.1 slice_reduce_fusion
  46.8 0.7 %reshape.11 = f32[4,8]{1,0:T(4,128)} reshape(f32[32]{0:T(128)S(1)} %slice_reduce_fusion) | data formatting | bytes 256 | tf_op jit(solution)/shard_map/reshape | solution.py:142
  (14 shorter events, 0.1 us)
Async XLA Ops:
  0.0 10.0 %collective-permute-start.5 = (bf16[32,768]{1,0:T(8,128)(2,1)}, bf16[32,768]{1,0:T(8,128)(2,1)S(1)}, u32[]{:S(2)}, u32[]{:S(2)}) collective-permute-start(bf16[32,768]{1,0:T(8,128)(2,1)} %bitcast.2), channel_id=1, source_target_pairs={{0,8},{1,9},{2,10},{3,11},{4,12},{5,13},{6,14},{7,15},{8,0},{9,1},... | collective-permute-start | bytes 147464 | tf_op jit(solution)/shard_map/ppermute | solution.py:33
  3.0 7.0 %collective-permute-start.6 = (bf16[32,768]{1,0:T(8,128)(2,1)}, bf16[32,768]{1,0:T(8,128)(2,1)S(1)}, u32[]{:S(2)}, u32[]{:S(2)}) collective-permute-start(bf16[32,768]{1,0:T(8,128)(2,1)} %bitcast.3), channel_id=1, source_target_pairs={{0,16},{1,17},{2,18},{3,19},{4,20},{5,21},{6,22},{7,23},{8,24},{9,... | collective-permute-start | bytes 147464 | tf_op jit(solution)/shard_map/ppermute | solution.py:33
  4.5 5.5 %collective-permute-start.7 = (bf16[32,768]{1,0:T(8,128)(2,1)}, bf16[32,768]{1,0:T(8,128)(2,1)S(1)}, u32[]{:S(2)}, u32[]{:S(2)}) collective-permute-start(bf16[32,768]{1,0:T(8,128)(2,1)} %bitcast.4), channel_id=1, source_target_pairs={{0,24},{1,25},{2,26},{3,27},{4,28},{5,29},{6,30},{7,31},{8,16},{9,... | collective-permute-start | bytes 147464 | tf_op jit(solution)/shard_map/ppermute | solution.py:33
  4.5 5.6 %collective-permute-start = (bf16[32,768]{1,0:T(8,128)(2,1)}, bf16[32,768]{1,0:T(8,128)(2,1)S(1)}, u32[]{:S(2)}, u32[]{:S(2)}) collective-permute-start(bf16[32,768]{1,0:T(8,128)(2,1)} %bitcast.5), channel_id=1, source_target_pairs={{0,1},{1,0},{2,3},{3,2},{4,5},{5,4},{6,7},{7,6},{8,9},{9,8},{10,11... | collective-permute-start | bytes 147464 | tf_op jit(solution)/shard_map/ppermute | solution.py:33
  6.5 6.1 %collective-permute-start.1 = (bf16[32,768]{1,0:T(8,128)(2,1)}, bf16[32,768]{1,0:T(8,128)(2,1)S(1)}, u32[]{:S(2)}, u32[]{:S(2)}) collective-permute-start(bf16[32,768]{1,0:T(8,128)(2,1)} %bitcast.6), channel_id=1, source_target_pairs={{0,2},{1,3},{2,0},{3,1},{4,6},{5,7},{6,4},{7,5},{8,10},{9,11},{10,... | collective-permute-start | bytes 147464 | tf_op jit(solution)/shard_map/ppermute | solution.py:33
  10.0 6.1 %collective-permute-start.2 = (bf16[32,768]{1,0:T(8,128)(2,1)}, bf16[32,768]{1,0:T(8,128)(2,1)S(1)}, u32[]{:S(2)}, u32[]{:S(2)}) collective-permute-start(bf16[32,768]{1,0:T(8,128)(2,1)} %bitcast.7), channel_id=1, source_target_pairs={{0,3},{1,2},{2,1},{3,0},{4,7},{5,6},{6,5},{7,4},{8,11},{9,10},{10,... | collective-permute-start | bytes 147464 | tf_op jit(solution)/shard_map/ppermute | solution.py:33
  16.1 6.5 %collective-permute-start.11 = (bf16[96,768]{1,0:T(8,128)(2,1)S(1)}, bf16[96,768]{1,0:T(8,128)(2,1)S(1)}, u32[]{:S(2)}, u32[]{:S(2)}) collective-permute-start(bf16[96,768]{1,0:T(8,128)(2,1)S(1)} %get-tuple-element.6), channel_id=1, source_target_pairs={{0,16},{1,17},{2,18},{3,19},{4,20},{5,21},{6,22},{7,23},{8,24},{9,... | collective-permute-start | bytes 442376 | tf_op jit(solution)/shard_map/ppermute | solution.py:33
  17.7 6.1 %collective-permute-start.9 = (bf16[96,768]{1,0:T(8,128)(2,1)S(1)}, bf16[96,768]{1,0:T(8,128)(2,1)S(1)}, u32[]{:S(2)}, u32[]{:S(2)}) collective-permute-start(bf16[96,768]{1,0:T(8,128)(2,1)S(1)} %get-tuple-element.6), channel_id=1, source_target_pairs={{0,8},{1,9},{2,10},{3,11},{4,12},{5,13},{6,14},{7,15},{8,0},{9,1},... | collective-permute-start | bytes 442376 | tf_op jit(solution)/shard_map/ppermute | solution.py:33
  19.2 10.2 %collective-permute-start.3 = (bf16[96,768]{1,0:T(8,128)(2,1)S(1)}, bf16[96,768]{1,0:T(8,128)(2,1)S(1)}, u32[]{:S(2)}, u32[]{:S(2)}) collective-permute-start(bf16[96,768]{1,0:T(8,128)(2,1)S(1)} %get-tuple-element.6), channel_id=1, source_target_pairs={{0,24},{1,25},{2,26},{3,27},{4,28},{5,29},{6,30},{7,31},{8,16},{9,... | collective-permute-start | bytes 442376 | tf_op jit(solution)/shard_map/ppermute | solution.py:33
  22.5 7.3 %collective-permute-start.12 = (bf16[96,768]{1,0:T(8,128)(2,1)S(1)}, bf16[96,768]{1,0:T(8,128)(2,1)S(1)}, u32[]{:S(2)}, u32[]{:S(2)}) collective-permute-start(bf16[96,768]{1,0:T(8,128)(2,1)S(1)} %collective-permute-done.11.refs_0_), channel_id=1, source_target_pairs={{0,4},{1,5},{2,6},{3,7},{4,0},{5,1},{6,2},{7,3},{8,12},{9,13},{10,... | collective-permute-start | bytes 442376 | tf_op jit(solution)/shard_map/ppermute | solution.py:33
  23.3 10.4 %collective-permute-start.8 = (bf16[224,768]{1,0:T(8,128)(2,1)S(1)}, bf16[224,768]{1,0:T(8,128)(2,1)S(1)}, u32[]{:S(2)}, u32[]{:S(2)}) collective-permute-start(bf16[224,768]{1,0:T(8,128)(2,1)S(1)} %get-tuple-element.5.refs_0_), channel_id=1, source_target_pairs={{0,4},{1,5},{2,6},{3,7},{4,0},{5,1},{6,2},{7,3},{8,12},{9,13},{10,... | collective-permute-start | bytes 1032200 | tf_op jit(solution)/shard_map/ppermute | solution.py:33
  23.8 8.0 %collective-permute-start.10 = (bf16[96,768]{1,0:T(8,128)(2,1)S(1)}, bf16[96,768]{1,0:T(8,128)(2,1)S(1)}, u32[]{:S(2)}, u32[]{:S(2)}) collective-permute-start(bf16[96,768]{1,0:T(8,128)(2,1)S(1)} %collective-permute-done.9.refs_0_), channel_id=1, source_target_pairs={{0,4},{1,5},{2,6},{3,7},{4,0},{5,1},{6,2},{7,3},{8,12},{9,13},{10,... | collective-permute-start | bytes 442376 | tf_op jit(solution)/shard_map/ppermute | solution.py:33
  23.9 2.8 %copy-start = (bf16[4096,768]{1,0:T(8,128)(2,1)S(1)}, bf16[4096,768]{1,0:T(8,128)(2,1)}, u32[]{:S(2)}) copy-start(bf16[4096,768]{1,0:T(8,128)(2,1)} %kept_ref.9) | copy-start | bytes 18874372
  26.7 0.8 %copy-start.1 = (bf16[4,8,768]{2,1,0:T(8,128)(2,1)S(1)}, bf16[4,8,768]{2,1,0:T(8,128)(2,1)}, u32[]{:S(2)}) copy-start(bf16[4,8,768]{2,1,0:T(8,128)(2,1)} %param.4) | copy-start | bytes 147460
  29.4 6.2 %collective-permute-start.4 = (bf16[96,768]{1,0:T(8,128)(2,1)S(1)}, bf16[96,768]{1,0:T(8,128)(2,1)S(1)}, u32[]{:S(2)}, u32[]{:S(2)}) collective-permute-start(bf16[96,768]{1,0:T(8,128)(2,1)S(1)} %collective-permute-done.3.refs_0_), channel_id=1, source_target_pairs={{0,4},{1,5},{2,6},{3,7},{4,0},{5,1},{6,2},{7,3},{8,12},{9,13},{10,... | collective-permute-start | bytes 442376 | tf_op jit(solution)/shard_map/ppermute | solution.py:33
